TPU v7x, 128 devices: a whole 4x4x4 slice. The times are simulated.
128 devices in a mesh: ctx: 8 (over z, y_hi), tp: 16 (over y_lo, x, core).
Axes of the slice: x: 4, y: 4 (y_hi: 2, y_lo: 2; y = y_hi * 2 + y_lo), z: 4, core: 2. Of those that a mesh axis runs over, the one named last changes fastest.
Arguments:
- byte_embeds: bfloat16 [24576, 1024], P(('ctx', 'tp')), may hold values from -6 to 6
- local_embeds: bfloat16 [24576, 1024], P(('ctx', 'tp')), may hold values from -6 to 6
- global_qkv: bfloat16 [3, 8192, 4096], P(None, None, 'tp'), may hold values from -0.0625 to 0.0625
- global_out: bfloat16 [4096, 8192], P('tp'), may hold values from -1.5 to 1.5
- local_qkv: bfloat16 [1, 1024, 3072], replicated, may hold values from -0.1875 to 0.1875
- local_out: bfloat16 [1, 1024, 1024], replicated, may hold values from -0.1875 to 0.1875
- cotangent: bfloat16 [24576, 1024], P(('ctx', 'tp')), may hold values from -6 to 6
Outputs:
- hidden: bfloat16 [24576, 1024], P(('ctx', 'tp'))
- grad_qkv: float32 [1, 1024, 3072], P(None, ('ctx', 'tp'))
- grad_out: float32 [1, 1024, 1024], P(None, ('ctx', 'tp'))
All inputs are finite; a program needn't handle non-finite values.
Results may differ from a plain program's by a relative error of at most 0.028.
Values may be sent and summed in bfloat16 or wider, within the bound.
A program may use at most 128 MiB of HBM per device.

v0:
```python
import math
import jax
import jax.numpy as jnp
from jax import lax
from jax.sharding import PartitionSpec as P

PATCH = 8
HEAD_DIM = 128
LOCAL_HEADS = 8
LOCAL_HEAD_DIM = 128


def from_behind(value, axis, steps):
    count = lax.axis_size(axis)
    initial, last = (max(0, -steps), min(count, count - steps))
    return lax.ppermute(value, axis, [(source, source + steps) for source in range(initial, last)])


def rms_norm(values):
    return values * lax.rsqrt(jnp.mean(values * values, axis=-1, keepdims=True) + 1e-06)


def local_core(qkv_rows):
    total = qkv_rows.shape[0]
    groups = total // PATCH
    width = qkv_rows.shape[1] // 3
    parts = qkv_rows.reshape(groups, PATCH, 3, LOCAL_HEADS, LOCAL_HEAD_DIM)
    queries = rms_norm(parts[:, :, 0])
    keys_all = rms_norm(parts[:, :, 1])
    values = parts[:, :, 2]
    scores = jnp.einsum("npha,nqha->nhpq", queries, keys_all) / math.sqrt(LOCAL_HEAD_DIM)
    causal = jnp.arange(PATCH)[:, None] >= jnp.arange(PATCH)[None, :]
    weights = jnp.where(causal[None, None], jnp.exp(scores), 0.0)
    numerator = jnp.einsum("nhpq,nqha->npha", weights, values)
    denominator = jnp.sum(weights, axis=-1).transpose(0, 2, 1)[..., None]
    return (numerator / denominator).reshape(total, width)


def local_pass(state, local_qkv, local_out, cotangent):
    layer = 0
    normed = rms_norm(state).astype(jnp.bfloat16)
    qkv_rows = jnp.dot(normed, local_qkv[layer], preferred_element_type=jnp.float32)
    core, core_back = jax.vjp(local_core, qkv_rows)
    attended = core.astype(jnp.bfloat16)
    saved = [(state, normed, core_back, attended)]
    state = state + jnp.dot(attended, local_out[layer], preferred_element_type=jnp.float32)
    hidden = state.astype(jnp.bfloat16)
    grad_state = cotangent.astype(jnp.float32)
    layer = 0
    before, normed, core_back, attended = saved[layer]
    grad_round = grad_state.astype(jnp.bfloat16)
    grads_out = [jnp.dot(attended.T, grad_round, preferred_element_type=jnp.float32)]
    grad_core = jnp.dot(grad_round, local_out[layer].T, preferred_element_type=jnp.float32)
    grad_rows = core_back(grad_core)[0].astype(jnp.bfloat16)
    grads_qkv = [jnp.dot(normed.T, grad_rows, preferred_element_type=jnp.float32)]
    return (hidden, jnp.stack(grads_qkv[::-1]), jnp.stack(grads_out[::-1]))


def per_device(byte_embeds, local_embeds, global_qkv, global_out, local_qkv, local_out, cotangent):
    byte_count = byte_embeds.shape[0]
    patch_count = byte_count // PATCH
    full_width = PATCH * byte_embeds.shape[1]
    patch_in = byte_embeds.reshape(patch_count, full_width).astype(jnp.float32)
    normed = rms_norm(patch_in).astype(jnp.bfloat16)
    projected = jnp.einsum(
        "nd,cdh->nch",
        lax.all_gather(normed, "tp", axis=0, tiled=True),
        global_qkv,
        preferred_element_type=jnp.float32,
    )
    shard_rows = projected.shape[0]
    head_width = global_qkv.shape[2]
    head_count = head_width // HEAD_DIM
    queries = rms_norm(projected[:, 0].reshape(shard_rows, head_count, HEAD_DIM)).astype(
        jnp.bfloat16
    )
    keys_mine = rms_norm(projected[:, 1].reshape(shard_rows, head_count, HEAD_DIM)).astype(
        jnp.bfloat16
    )
    values_mine = projected[:, 2].reshape(shard_rows, head_count, HEAD_DIM).astype(jnp.bfloat16)
    query_pos = lax.axis_index("ctx") * shard_rows + jnp.arange(shard_rows, dtype=jnp.int32)
    key_piece = lax.all_gather(keys_mine, "ctx", axis=0, tiled=True)
    value_piece = lax.all_gather(values_mine, "ctx", axis=0, tiled=True)
    key_count = key_piece.shape[0]
    scores = jnp.einsum(
        "rha,kha->rhk", queries, key_piece, preferred_element_type=jnp.float32
    ) / math.sqrt(HEAD_DIM)
    key_pos = jnp.arange(key_count, dtype=jnp.int32)
    allowed = key_pos[None, None, :] <= query_pos[:, None, None]
    expo = jnp.where(allowed, jnp.exp(scores), 0.0)
    numerator = jnp.einsum(
        "rhk,kha->rha", expo.astype(jnp.bfloat16), value_piece, preferred_element_type=jnp.float32
    )
    denominator = jnp.sum(expo, axis=-1)
    numerator, denominator = (numerator, denominator)
    attended = (
        (numerator / denominator[..., None]).reshape(shard_rows, head_width).astype(jnp.bfloat16)
    )
    patch_out = lax.psum_scatter(
        jnp.dot(attended, global_out, preferred_element_type=jnp.float32).astype(jnp.bfloat16),
        "tp",
        scatter_dimension=0,
        tiled=True,
    )
    earlier_row = from_behind(patch_out[-1:], ("ctx", "tp"), 1)
    patch_out = jnp.concatenate([earlier_row, patch_out[:-1]], axis=0)
    context = patch_out.reshape(byte_count, byte_embeds.shape[1])
    state = local_embeds.astype(jnp.float32) + context.astype(jnp.float32)
    hidden, grad_qkv, grad_out = local_pass(state, local_qkv, local_out, cotangent)
    grad_qkv, grad_out = (
        lax.psum_scatter(grad_qkv, ("ctx", "tp"), scatter_dimension=1, tiled=True),
        lax.psum_scatter(grad_out, ("ctx", "tp"), scatter_dimension=1, tiled=True),
    )
    return (hidden, grad_qkv, grad_out)


def solution(mesh):
    in_specs = (
        P(("ctx", "tp"), None),
        P(("ctx", "tp"), None),
        P(None, None, "tp"),
        P("tp", None),
        P(),
        P(),
        P(("ctx", "tp"), None),
    )
    out_specs = (P(("ctx", "tp"), None), P(None, ("ctx", "tp"), None), P(None, ("ctx", "tp"), None))
    return jax.shard_map(
        per_device, mesh=mesh, in_specs=in_specs, out_specs=out_specs, check_vma=False
    )
```

profile of v0, /device:TPU:0, one launch (start us, length us, event | category | flops | bytes accessed | tf_op | source)
XLA Modules:
  0.0 1156.8 jit_solution(7614287349965638369)
XLA Ops:
  7.2 1.3 reshape.139
  8.5 1.2 multiply_reduce_fusion.6
  10.8 44.9 %all-gather.4.cloned.1.call-done = bf16[384,8192]{1,0:T(8,128)(2,1)} async-done(((bf16[24,8192]{1,0:T(8,128)(2,1)}), bf16[384,8192]{1,0:T(8,128)(2,1)}) %all-gather.4.cloned.1.call-update) | async-done | bytes 6291472 | tf_op jit(solution)/shard_map/all_gather | solution.py:67
  55.8 11.2 fusion.2
  67.1 0.9 copy-done.16
  69.2 1.7 slice.71
  70.9 2.0 iota_compare_fusion
  73.9 45.5 %all-gather.8.cloned.1.call-done = bf16[3072,2,128]{2,0,1:T(8,128)(2,1)} async-done(((bf16[384,2,128]{2,0,1:T(8,128)(2,1)}), bf16[3072,2,128]{2,0,1:T(8,128)(2,1)}) %all-gather.8.cloned.1.call-update) | async-done | bytes 1572880 | tf_op jit(solution)/shard_map/all_gather | solution.py:82
  119.4 7.9 fusion
  127.3 42.8 %all-gather.6.cloned.1.call-done = bf16[3072,2,128]{0,2,1:T(8,128)(2,1)} async-done(((bf16[384,2,128]{0,2,1:T(8,128)(2,1)}), bf16[3072,2,128]{0,2,1:T(8,128)(2,1)}) %all-gather.6.cloned.1.call-update) | async-done | bytes 1572880 | tf_op jit(solution)/shard_map/all_gather | solution.py:83
  170.1 6.6 fusion.27
  176.7 4.5 convolution_convert_fusion
  182.1 1.7 fusion.38
  183.9 66.3 %reduce-scatter.4.cloned.1.call-done = bf16[24,8192]{1,0:T(8,128)(2,1)} async-done(((bf16[384,8192]{1,0:T(8,128)(2,1)}), bf16[24,8192]{1,0:T(8,128)(2,1)}) %reduce-scatter.4.cloned.1.call-update) | async-done | bytes 393232 | tf_op jit(solution)/shard_map/reduce_scatter | solution.py:99
  251.1 1.5 collective-permute-start
  252.6 8.7 copy.36
  261.3 1.0 maximum_convert_fusion
  262.2 1.3 reshape.140
  263.7 1.1 multiply_convert_fusion
  264.8 4.3 fusion.40
  271.1 1.3 multiply_reduce_fusion.2
  273.3 3.2 convolution_bitcast_fusion.1
  276.6 1.1 negate_bitcast_fusion
  277.7 2.1 fusion.16
  281.9 1.0 fusion.30
  283.2 1.2 copy.28
  284.5 3.0 convert_element_type.83
  287.5 7.7 convolution_bitcast_fusion
  295.1 1.0 copy-done.8
  296.1 2.5 fusion.18
  298.6 630.3 %reduce-scatter.8.cloned.1.call-done = f32[1,8,1024]{2,1,0:T(8,128)} async-done(((f32[1,1024,1024]{2,1,0:T(8,128)}), f32[1,8,1024]{2,1,0:T(8,128)}) %reduce-scatter.8.cloned.1.call-update) | async-done | bytes 32784 | tf_op jit(solution)/shard_map/reduce_scatter | solution.py:112
  928.9 221.0 %reduce-scatter.6.cloned.1.call-done = f32[1,8,3072]{2,1,0:T(8,128)} async-done(((f32[1,1024,3072]{2,1,0:T(8,128)}), f32[1,8,3072]{2,1,0:T(8,128)}) %reduce-scatter.6.cloned.1.call-update) | async-done | bytes 98320 | tf_op jit(solution)/shard_map/reduce_scatter | solution.py:111
  (84 shorter events, 10.6 us)
Async XLA Ops:
  7.2 174.1 %copy-start = (bf16[1,1024,1024]{2,1,0:T(8,128)(2,1)S(1)}, bf16[1,1024,1024]{2,1,0:T(8,128)(2,1)}, u32[]{:S(2)}) copy-start(bf16[1,1024,1024]{2,1,0:T(8,128)(2,1)} %param.12) | copy-start | bytes 6291460
  7.2 48.6 %all-gather.4.cloned.1.call-start = ((), (), s32[]{:S(2)}) async-start(), calls=%async_computation.3 | async-start | bytes 6684672 | tf_op jit(solution)/shard_map/all_gather | solution.py:67
  10.8 108.7 %all-gather.8.cloned.1.call-start = ((), (), s32[]{:S(2)}) async-start(), calls=%async_computation.5 | async-start | bytes 1769472 | tf_op jit(solution)/shard_map/all_gather | solution.py:82
  67.0 1.0 copy-start.16
  69.1 101.0 %all-gather.6.cloned.1.call-start = ((), (), s32[]{:S(2)}) async-start(), calls=%async_computation.4 | async-start | bytes 1769472 | tf_op jit(solution)/shard_map/all_gather | solution.py:83
  70.9 179.3 %reduce-scatter.4.cloned.1.call-start = ((), (), s32[]{:S(2)}) async-start(), calls=%async_computation.6 | async-start | bytes 6684672 | tf_op jit(solution)/shard_map/reduce_scatter | solution.py:99
  73.9 96.2 %copy-start.11 = (pred[384,3072]{0,1:T(8,128)(4,1)S(1)}, pred[384,3072]{0,1:T(8,128)(4,1)}, u32[]{:S(2)}) copy-start(pred[384,3072]{0,1:T(8,128)(4,1)} %iota_compare_fusion) | copy-start | bytes 3538948
  170.1 6.6 copy-start.3
  181.1 1.0 copy-start.9
  181.2 747.8 %reduce-scatter.8.cloned.1.call-start = ((), (), s32[]{:S(2)}) async-start(), calls=%async_computation.8 | async-start | bytes 4227072 | tf_op jit(solution)/shard_map/reduce_scatter | solution.py:112
  251.1 10.2 collective-permute-start
  252.6 8.7 copy-start.19
  261.2 2.3 copy-start.7
  269.1 1.9 copy-start.1
  269.2 1.9 copy-start.4
  269.6 0.6 copy-start.14
  269.7 0.7 copy-start.12
  271.0 1.4 copy-start.17
  271.0 1.4 copy-start.20
  271.0 2.3 copy-start.10
  272.4 0.9 copy-start.6
  276.6 873.4 %reduce-scatter.6.cloned.1.call-start = ((), (), s32[]{:S(2)}) async-start(), calls=%async_computation.7 | async-start | bytes 12681216 | tf_op jit(solution)/shard_map/reduce_scatter | solution.py:111
  276.6 3.2 copy-start.2
  279.8 1.6 copy-start.13
  279.8 1.6 copy-start.15
  279.8 1.6 copy-start.5
  279.8 1.6 copy-start.18
  279.8 1.6 copy-start.21
  295.1 1.0 copy-start.8
  295.1 1.0 copy-start.22
Sparse Core Ops, SparseCore 0:
  10.9 44.7 all-gather.3
  69.2 50.1 all-gather.7
  121.6 48.4 all-gather.5
  181.3 68.7 reduce-scatter.3
  276.7 652.2 reduce-scatter.7
  934.4 215.5 reduce-scatter.5
where the time goes:
time: 1160 us
  waiting for transfers between devices  1050 us (91%)
  matrix products  55.6 us (5%)
  local copies, waits for them, and re-layouts  23.8 us (2%)
  between operations  14.5 us (1%)
    reduce_scatter x1, waiting for transfers between devices, per_device(): lax.psum_scatter(grad_out, ('ctx', 'tp'), scatter_dimension=1, tiled=True)  630 us
    reduce_scatter x1, waiting for transfers between devices, per_device(): lax.psum_scatter(grad_qkv, ('ctx', 'tp'), scatter_dimension=1, tiled=True)  221 us
    reduce_scatter x1, waiting for transfers between devices, per_device(): lax.psum_scatter(jnp.dot(attended, global_out, preferred_element_type=jnp...  66.3 us
    all_gather x1, waiting for transfers between devices, per_device(): key_piece = lax.all_gather(keys_mine, 'ctx', axis=0, tiled=True)  45.5 us
    all_gather x1, waiting for transfers between devices, per_device(): lax.all_gather(normed, 'tp', axis=0, tiled=True)  44.9 us
    all_gather x1, waiting for transfers between devices, per_device(): value_piece = lax.all_gather(values_mine, 'ctx', axis=0, tiled=True)  42.8 us
  transfers between devices with their start and end apart: 7, of which 6 were waited for; matrix products, arithmetic and copies ran while one was open for 4% of the time, Pallas kernels for 0%

commit v1 on v0

--- a/solution.py
+++ b/solution.py
@@ -79,7 +79,9 @@
     )
     values_mine = projected[:, 2].reshape(shard_rows, head_count, HEAD_DIM).astype(jnp.bfloat16)
     query_pos = lax.axis_index("ctx") * shard_rows + jnp.arange(shard_rows, dtype=jnp.int32)
-    key_piece = lax.all_gather(keys_mine, "ctx", axis=0, tiled=True)
+    key_piece = jnp.concatenate(
+        lax.all_to_all(jnp.stack([keys_mine] * lax.axis_size("ctx")), "ctx", 0, 0), axis=0
+    )
     value_piece = lax.all_gather(values_mine, "ctx", axis=0, tiled=True)
     key_count = key_piece.shape[0]
     scores = jnp.einsum(

time: 1160 us -> 1120 us (0.966)
  waiting for transfers between devices: 1050 us -> 1000 us
    all_gather x1 -> x0, waiting for transfers between devices: 45.5 us -> none  [per_device(): key_piece = lax.all_gather(keys_mine, 'ctx', axis=0, tiled=True)]
    all_gather x1, waiting for transfers between devices: 42.8 us -> 18.3 us  [per_device(): value_piece = lax.all_gather(values_mine, 'ctx', axis=0, tiled=True)]
    all_to_all x0 -> x1, waiting for transfers between devices: none -> 22.6 us  [per_device(): lax.all_to_all(jnp.stack([keys_mine] * lax.axis_size('ctx')), 'ctx', 0, 0)]
where the time goes in v1:
time: 1120 us
  waiting for transfers between devices  1000 us (89%)
  matrix products  52.7 us (5%)
  local copies, waits for them, and re-layouts  27 us (2%)
  between operations  14.2 us (1%)
    reduce_scatter x1, waiting for transfers between devices, per_device(): lax.psum_scatter(grad_out, ('ctx', 'tp'), scatter_dimension=1, tiled=True)  630 us
    reduce_scatter x1, waiting for transfers between devices, per_device(): lax.psum_scatter(grad_qkv, ('ctx', 'tp'), scatter_dimension=1, tiled=True)  221 us
    reduce_scatter x1, waiting for transfers between devices, per_device(): lax.psum_scatter(jnp.dot(attended, global_out, preferred_element_type=jnp...  66.3 us
    all_gather x1, waiting for transfers between devices, per_device(): lax.all_gather(normed, 'tp', axis=0, tiled=True)  44.9 us
    all_to_all x1, waiting for transfers between devices, per_device(): lax.all_to_all(jnp.stack([keys_mine] * lax.axis_size('ctx')), 'ctx', 0, 0)  22.6 us
  transfers between devices with their start and end apart: 7, of which 6 were waited for; matrix products, arithmetic and copies ran while one was open for 4% of the time, Pallas kernels for 0%

profile of v1, /device:TPU:0, one launch (start us, length us, event | category | flops | bytes accessed | tf_op | source)
XLA Modules:
  0.0 1115.3 jit_solution(13372892510777114004)
XLA Ops:
  7.2 1.3 reshape.146
  8.5 1.2 multiply_reduce_fusion.6
  10.8 44.9 %all-gather.3.cloned.1.call-done = bf16[384,8192]{1,0:T(8,128)(2,1)} async-done(((bf16[24,8192]{1,0:T(8,128)(2,1)}), bf16[384,8192]{1,0:T(8,128)(2,1)}) %all-gather.3.cloned.1.call-update) | async-done | bytes 6291472 | tf_op jit(solution)/shard_map/all_gather | solution.py:67
  55.8 11.2 %fusion.2 = f32[384,3,256]{0,2,1:T(8,128)S(1)} fusion(bf16[3,8192,256]{2,1,0:T(8,128)(2,1)} %param.9, bf16[384,8192]{1,0:T(8,128)(2,1)} %all-gather.3.cloned.1.call-done), kind=kOutput, calls=%fused_computation.5 | convolution fusion | flops 4831838208 | bytes 20054016 | tf_op jit(solution)/shard_map/nd,cdh->nch/dot_general | solution.py:65
  68.7 1.2 fusion.60
  70.2 1.5 stack.6
  71.6 6.6 all-to-all-start
  78.3 1.9 iota_compare_fusion
  81.3 22.6 %all-to-all-done = bf16[8,384,2,128]{3,1,2,0:T(8,128)(2,1)} async-done(((bf16[8,384,2,128]{3,1,2,0:T(8,128)(2,1)}), bf16[8,384,2,128]{3,1,2,0:T(8,128)(2,1)}, u32[]{:S(2)}, u32[]{:S(2)}) %all-to-all-start) | async-done | bytes 1572896 | tf_op jit(solution)/shard_map/all_to_all | solution.py:83
  103.9 1.6 copy.31
  105.5 5.0 fusion
  110.5 18.3 %all-gather.5.cloned.1.call-done = bf16[3072,2,128]{0,2,1:T(8,128)(2,1)} async-done(((bf16[384,2,128]{0,2,1:T(8,128)(2,1)}), bf16[3072,2,128]{0,2,1:T(8,128)(2,1)}) %all-gather.5.cloned.1.call-update) | async-done | bytes 1572880 | tf_op jit(solution)/shard_map/all_gather | solution.py:85
  128.8 6.5 fusion.27
  135.4 4.5 convolution_convert_fusion
  140.9 1.7 fusion.38
  142.6 66.3 %reduce-scatter.4.cloned.1.call-done = bf16[24,8192]{1,0:T(8,128)(2,1)} async-done(((bf16[384,8192]{1,0:T(8,128)(2,1)}), bf16[24,8192]{1,0:T(8,128)(2,1)}) %reduce-scatter.4.cloned.1.call-update) | async-done | bytes 393232 | tf_op jit(solution)/shard_map/reduce_scatter | solution.py:101
  209.8 1.5 collective-permute-start
  211.3 8.7 copy.47
  221.0 1.3 reshape.147
  222.5 1.1 multiply_convert_fusion
  223.6 4.3 fusion.40
  229.8 1.3 multiply_reduce_fusion.2
  232.1 3.2 convolution_bitcast_fusion.1
  235.4 1.1 negate_bitcast_fusion
  236.4 2.1 fusion.16
  240.7 1.0 fusion.30
  241.9 1.2 copy.39
  243.2 3.0 convert_element_type.85
  246.2 7.7 convolution_bitcast_fusion
  254.8 2.5 fusion.18
  257.4 630.3 %reduce-scatter.8.cloned.1.call-done = f32[1,8,1024]{2,1,0:T(8,128)} async-done(((f32[1,1024,1024]{2,1,0:T(8,128)}), f32[1,8,1024]{2,1,0:T(8,128)}) %reduce-scatter.8.cloned.1.call-update) | async-done | bytes 32784 | tf_op jit(solution)/shard_map/reduce_scatter | solution.py:114
  887.7 221.1 %reduce-scatter.6.cloned.1.call-done = f32[1,8,3072]{2,1,0:T(8,128)} async-done(((f32[1,1024,3072]{2,1,0:T(8,128)}), f32[1,8,3072]{2,1,0:T(8,128)}) %reduce-scatter.6.cloned.1.call-update) | async-done | bytes 98320 | tf_op jit(solution)/shard_map/reduce_scatter | solution.py:113
  (87 shorter events, 13.4 us)
Async XLA Ops:
  7.2 132.8 %copy-start = (bf16[1,1024,1024]{2,1,0:T(8,128)(2,1)S(1)}, bf16[1,1024,1024]{2,1,0:T(8,128)(2,1)}, u32[]{:S(2)}) copy-start(bf16[1,1024,1024]{2,1,0:T(8,128)(2,1)} %param.12) | copy-start | bytes 6291460
  7.2 48.6 %all-gather.3.cloned.1.call-start = ((), (), s32[]{:S(2)}) async-start(), calls=%async_computation.4 | async-start | bytes 6684672 | tf_op jit(solution)/shard_map/all_gather | solution.py:67
  10.8 118.0 %all-gather.5.cloned.1.call-start = ((), (), s32[]{:S(2)}) async-start(), calls=%async_computation.5 | async-start | bytes 1769472 | tf_op jit(solution)/shard_map/all_gather | solution.py:85
  67.0 1.0 copy-start.16
  71.6 32.2 %all-to-all-start = ((bf16[8,384,2,128]{3,1,2,0:T(8,128)(2,1)}), bf16[8,384,2,128]{3,1,2,0:T(8,128)(2,1)}, u32[]{:S(2)}, u32[]{:S(2)}) async-start(bf16[8,384,2,128]{3,1,2,0:T(8,128)(2,1)} %stack.6), calls=%async_computation | async-start | bytes 3145728 | tf_op jit(solution)/shard_map/all_to_all | solution.py:83
  78.3 130.6 %reduce-scatter.4.cloned.1.call-start = ((), (), s32[]{:S(2)}) async-start(), calls=%async_computation.6 | async-start | bytes 6684672 | tf_op jit(solution)/shard_map/reduce_scatter | solution.py:101
  81.2 24.2 %copy-start.11 = (pred[384,3072]{0,1:T(8,128)(4,1)S(1)}, pred[384,3072]{0,1:T(8,128)(4,1)}, u32[]{:S(2)}) copy-start(pred[384,3072]{0,1:T(8,128)(4,1)} %iota_compare_fusion) | copy-start | bytes 3538948
  103.9 1.6 copy-start.20
  128.8 6.6 copy-start.3
  139.9 1.0 copy-start.9
  139.9 747.8 %reduce-scatter.8.cloned.1.call-start = ((), (), s32[]{:S(2)}) async-start(), calls=%async_computation.8 | async-start | bytes 4227072 | tf_op jit(solution)/shard_map/reduce_scatter | solution.py:114
  209.8 10.2 collective-permute-start
  211.3 8.7 copy-start.19
  220.0 2.3 copy-start.7
  227.9 1.9 copy-start.1
  227.9 1.9 copy-start.4
  228.4 0.6 copy-start.14
  228.4 0.7 copy-start.12
  229.7 1.4 copy-start.17
  229.7 1.4 copy-start.21
  229.7 2.3 copy-start.10
  231.1 0.9 copy-start.6
  235.3 873.4 %reduce-scatter.6.cloned.1.call-start = ((), (), s32[]{:S(2)}) async-start(), calls=%async_computation.7 | async-start | bytes 12681216 | tf_op jit(solution)/shard_map/reduce_scatter | solution.py:113
  235.3 3.2 copy-start.2
  238.5 1.6 copy-start.13
  238.5 1.6 copy-start.15
  238.6 1.6 copy-start.5
  238.6 1.6 copy-start.18
  238.6 1.6 copy-start.22
  253.8 1.0 copy-start.8
  253.8 1.0 copy-start.23
Sparse Core Ops, SparseCore 0:
  10.9 44.7 all-gather.2
  68.9 59.9 all-gather.4
  140.0 68.7 reduce-scatter.3
  235.4 652.2 reduce-scatter.7
  893.1 215.6 reduce-scatter.5
